TPU v7x, 32 devices: a whole 2x2x4 slice. The times are simulated.
32 devices in a mesh: group: 2 (over y), seq: 4 (over z), shard: 2 (over x), guide: 2 (over core).
Axes of the slice: x: 2, y: 2, z: 4, core: 2. Of those that a mesh axis runs over, the one named last changes fastest.
Arguments:
- queries: bfloat16 [2, 2, 512, 2560], P('guide', 'group', 'seq', 'shard'), parts along dimension 1, may hold values from -120 to 120
- key_vecs: bfloat16 [2, 2, 512, 2560], P('guide', 'group', 'seq', 'shard'), parts along dimension 1, may hold values from -4 to 4
- value_vecs: bfloat16 [2, 2, 512, 2560], P('guide', 'group', 'seq', 'shard'), parts along dimension 1, may hold values from -24 to 24
- residual: bfloat16 [2, 2, 512, 5120], P('guide', 'group', 'seq', 'shard'), parts along dimension 1, may hold values from -64 to 64
- w_out: bfloat16 [2560, 5120], P('shard', 'guide'), may hold values from -0.125 to 0.125
- attn_gate: float32 [2, 5120], P('group', 'shard'), parts along dimension 0, may hold values from 2 to 4
- norm_shift: float32 [2, 5120], P('group', 'shard'), parts along dimension 0, may hold values from -3 to 3
- norm_scale: float32 [2, 5120], P('group', 'shard'), parts along dimension 0, may hold values from -2.5 to 2.5
- w_head: bfloat16 [5120, 64], P('shard'), may hold values from -0.078125 to 0.078125
- noise: float32 [2, 4, 128, 64], P('group', 'seq', None, 'guide'), parts along dimension 0, may hold values from -6 to 6
- timesteps: int32 [2], P('group'), parts along dimension 0, may hold values from 100 to 980
- frame_owner: int32 [2, 4], P('group'), parts along dimension 0, may hold values from 0 to 3, each once within a row
Outputs:
- sds_grad: float32 [2, 4, 128, 64], P('group', 'seq', None, 'guide'), parts along dimension 0
There are 2 independent parts, one for each index of `group`. A program takes and returns all parts, laid end to end along the dimension named above; an argument that names none is the same for every part. Nothing has to cross between parts.
Inputs may be any that keep to these rules, and one draw needn't show every extreme that they name: `frame_owner`: each row names every owner index once.
All inputs are finite; a program needn't handle non-finite values.
Results may differ from a plain program's by a relative error of at most 0.003.
Values may be sent and summed in bfloat16 or wider, within the bound.
No kernel may reach another device: no remote copies, remote signals or barrier semaphores. Data moves between devices by JAX's collectives and lax.ppermute only.
A program may use at most 128 MiB of HBM per device.

v0:
```python
import jax
import jax.numpy as jnp
from jax import lax
from jax.sharding import PartitionSpec as P

D = 5120
HEAD_DIM = 128
beta_low = 0.0001
beta_high = 0.02
guidance_scale = 3.0
norm_epsilon = 1e-06


def plan_weight(timesteps):
    steps_float = timesteps.astype(jnp.float32)
    exponent = (steps_float + 1.0) * beta_low + (beta_high - beta_low) * steps_float * (
        steps_float + 1.0
    ) / (2.0 * 999.0)
    return 1.0 - jnp.exp(-exponent)


def softmax_absorb(query_block, carry_state, pieces):
    running_top, running_total, running_acc = carry_state
    keys_block, values_block = pieces
    heads_local = query_block.shape[2]
    keys_split = keys_block.reshape(keys_block.shape[0], keys_block.shape[1], heads_local, HEAD_DIM)
    values_split = values_block.reshape(
        values_block.shape[0], values_block.shape[1], heads_local, HEAD_DIM
    )
    scores = jnp.einsum(
        "tqhd,tkhd->tqhk", query_block, keys_split, preferred_element_type=jnp.float32
    ) * HEAD_DIM ** (-0.5)
    new_top = jnp.max(scores, axis=-1)
    factor = jnp.exp(running_top - new_top)
    expo = jnp.exp(scores - new_top[..., None])
    new_total = running_total * factor + jnp.sum(expo, axis=-1)
    update = jnp.einsum(
        "tqhk,tkhd->tqhd",
        expo.astype(jnp.bfloat16),
        values_split,
        preferred_element_type=jnp.float32,
    )
    return (new_top, new_total, running_acc * factor[..., None] + update)


def start_state(step_count, token_count, heads_local):
    return (
        jnp.full((step_count, token_count, heads_local), -jnp.inf, jnp.float32),
        jnp.zeros((step_count, token_count, heads_local), jnp.float32),
        jnp.zeros((step_count, token_count, heads_local, HEAD_DIM), jnp.float32),
    )


def on_device(
    queries,
    key_vecs,
    value_vecs,
    residual,
    w_out,
    attn_gate,
    norm_shift,
    norm_scale,
    w_head,
    noise,
    timesteps,
    frame_owner,
):
    query_local = queries[0]
    step_count, token_count, width_local = query_local.shape
    heads_local = width_local // HEAD_DIM
    query_split = query_local.reshape(step_count, token_count, heads_local, HEAD_DIM)
    final_state = softmax_absorb(
        query_split,
        start_state(step_count, token_count, heads_local),
        (
            lax.all_gather(key_vecs[0], "seq", axis=1, tiled=True),
            lax.all_gather(value_vecs[0], "seq", axis=1, tiled=True),
        ),
    )
    total_sum = final_state[1]
    acc_sum = final_state[2]
    row_count = step_count * token_count
    attended = (acc_sum / total_sum[..., None]).astype(jnp.bfloat16).reshape(row_count, width_local)
    both_rows = jnp.dot(
        lax.all_gather(attended, "guide", axis=0, tiled=True),
        w_out,
        preferred_element_type=jnp.float32,
    )
    half_width = w_out.shape[1]
    swapped = lax.all_to_all(
        both_rows.reshape(2, row_count, half_width),
        "guide",
        split_axis=0,
        concat_axis=2,
        tiled=True,
    )
    projected = swapped.reshape(row_count, 2 * half_width)
    attn_out = lax.psum_scatter(projected, "shard", scatter_dimension=1, tiled=True)
    width_shard = attn_out.shape[1]
    hidden = residual[0].astype(jnp.float32) + attn_gate[:, None, :] * attn_out.reshape(
        step_count, token_count, width_shard
    )
    sum_first = jnp.sum(hidden, axis=-1)
    sum_second = jnp.sum(hidden * hidden, axis=-1)
    sum_first, sum_second = lax.psum((sum_first, sum_second), "shard")
    mean_row = sum_first / D
    var_row = sum_second / D - mean_row * mean_row
    inv_std = lax.rsqrt(var_row + norm_epsilon)
    modulated = (hidden - mean_row[..., None]) * inv_std[..., None] * (
        1.0 + norm_scale[:, None, :]
    ) + norm_shift[:, None, :]
    head_float = w_head.astype(jnp.float32)
    partial_head = jnp.einsum("tqd,dc->tqc", modulated, head_float, precision=lax.Precision.HIGHEST)
    predicted = lax.psum(partial_head, "shard")
    seq_count = lax.axis_size("seq")
    frame_group = token_count // seq_count
    channels = predicted.shape[-1]
    frames_view = predicted.reshape(step_count, seq_count, frame_group, channels)
    owner_table = (
        frame_owner[:, :, None] == jnp.arange(seq_count, dtype=jnp.int32)[None, None, :]
    ).astype(jnp.float32)
    by_owner = jnp.einsum(
        "tfo,tfgc->togc", owner_table, frames_view, precision=lax.Precision.HIGHEST
    )
    weight = plan_weight(timesteps)
    arrived = lax.all_to_all(
        lax.all_to_all(by_owner[None], "seq", split_axis=2, concat_axis=3, tiled=True),
        "guide",
        split_axis=4,
        concat_axis=0,
        tiled=True,
    )
    guided = arrived[1] + guidance_scale * (arrived[0] - arrived[1])
    return weight[:, None, None, None] * (guided - noise)


def solution(mesh):
    return jax.shard_map(
        on_device,
        mesh=mesh,
        in_specs=(
            P("guide", "group", "seq", "shard"),
            P("guide", "group", "seq", "shard"),
            P("guide", "group", "seq", "shard"),
            P("guide", "group", "seq", "shard"),
            P("shard", "guide"),
            P("group", "shard"),
            P("group", "shard"),
            P("group", "shard"),
            P("shard", None),
            P("group", "seq", None, "guide"),
            P("group"),
            P("group", None),
        ),
        out_specs=P("group", "seq", None, "guide"),
        check_vma=False,
    )
```

profile of v0, /device:TPU:0, one launch (start us, length us, event | category | flops | bytes accessed | tf_op | source)
XLA Modules:
  0.0 175.5 jit_solution(11851235863250960437)
XLA Ops:
  6.5 0.0 copy-start
  6.5 0.0 copy-start.3
  6.5 0.0 all-gather.5.cloned.1.call-start
  6.5 1.9 %copy.44 = bf16[1,1,128,1280]{2,3,1,0:T(8,128)(2,1)} copy(bf16[1,1,128,1280]{3,2,1,0:T(8,128)(2,1)} %param.13) | data formatting | bytes 655360 | tf_op args[1]
  8.5 0.0 all-gather.5.cloned.1.call-update
  8.5 0.0 all-gather.7.cloned.1.call-start
  8.5 0.7 all-gather.7.cloned.1.call-update
  9.2 0.0 reduce-scatter.2.cloned.1.call-start
  9.3 0.0 copy-done.3
  9.3 0.2 copy.45
  9.5 35.6 %all-gather.5.cloned.1.call-done = bf16[1,1,512,1280]{2,3,1,0:T(8,128)(2,1)} async-done(((bf16[1,1,128,1280]{2,3,1,0:T(8,128)(2,1)}), bf16[1,1,512,1280]{2,3,1,0:T(8,128)(2,1)}) %all-gather.5.cloned.1.call-update) | async-done | bytes 1310736 | tf_op jit(solution)/shard_map/all_gather | solution.py:76
  45.1 1.9 %bitcast_reduce_fusion = (f32[128,10]{0,1:T(8,128)S(1)}, f32[10,512,128]{2,1,0:T(8,128)S(1)}) fusion(bf16[512,10,128]{0,2,1:T(8,128)(2,1)} %bitcast.120, bf16[128,10,128]{0,2,1:T(8,128)(2,1)S(1)} %bitcast.119), kind=kOutput, calls=%fused_computation.1 | convolution fusion | flops 169081600 | bytes 4264960 | tf_op jit(solution)/shard_map/tqhd,tkhd->tqhk/dot_general | solution.py:30
  47.0 0.4 fusion.1
  47.5 30.0 %all-gather.7.cloned.1.call-done = bf16[1,1,512,1280]{3,2,1,0:T(8,128)(2,1)} async-done(((bf16[1,1,128,1280]{3,2,1,0:T(8,128)(2,1)}), bf16[1,1,512,1280]{3,2,1,0:T(8,128)(2,1)}) %all-gather.7.cloned.1.call-update) | async-done | bytes 1310736 | tf_op jit(solution)/shard_map/all_gather | solution.py:77
  77.5 2.4 %copy.48 = bf16[1,1,512,1280]{2,3,1,0:T(8,128)(2,1)} copy(bf16[1,1,512,1280]{3,2,1,0:T(8,128)(2,1)} %all-gather.7.cloned.1.call-done) | data formatting | bytes 2621440 | tf_op jit(solution)/shard_map/all_gather | solution.py:77
  79.9 2.1 %fusion.22 = bf16[1,128,10,128]{1,3,2,0:T(8,128)(2,1)S(1)} fusion(bf16[512,10,128]{0,2,1:T(8,128)(2,1)} %bitcast.121, f32[10,512,128]{2,1,0:T(8,128)S(1)} %get-tuple-element.14, f32[128,10]{0,1:T(8,128)S(1)} %get-tuple-element.13, f32[128,10]{0,1:T(8,128)S(1)} %get-tuple-element.10, f32[128,10]{0,1:T(8,128)S(1)} %get-tuple-element.9), kind=kOutput, calls=%fused_computation.19 | convolution fusion | flops 170229760 | bytes 4275200 | tf_op jit(solution)/shard_map/tqhk,tkhd->tqhd/dot_general | solution.py:37
  82.0 2.3 %all_gather.11 = bf16[256,1280]{0,1:T(8,128)(2,1)S(1)} all-gather(bf16[128,1280]{0,1:T(8,128)(2,1)S(1)} %bitcast.122), channel_id=1, replica_groups=mesh['group'=2,'seq'=4,'shard'=2,'guide'=2] {'guide'}, dimensions={0}, use_global_device_ids=true | all-gather | bytes 983040 | tf_op jit(solution)/shard_map/all_gather | solution.py:85
  84.3 4.7 %fusion.40 = f32[256,2560]{1,0:T(8,128)S(1)} fusion(bf16[256,1280]{0,1:T(8,128)(2,1)S(1)} %all_gather.11, bf16[1280,2560]{1,0:T(8,128)(2,1)} %param.16), kind=kOutput, calls=%fused_computation.43 | convolution fusion | flops 1677721600 | bytes 9830400 | tf_op jit(solution)/shard_map/dot_general | solution.py:84
  89.1 5.8 %all_to_all.42 = f32[2,128,2560]{2,1,0:T(8,128)S(1)} all-to-all(f32[2,128,2560]{2,1,0:T(8,128)S(1)} %bitcast.115), channel_id=1, replica_groups=mesh['group'=2,'seq'=4,'shard'=2,'guide'=2] {'guide'}, dimensions={0} | all-to-all | bytes 5242880 | tf_op jit(solution)/shard_map/all_to_all | solution.py:90
  94.9 2.0 %copy.50 = f32[1,128,2,2560]{3,2,1,0:T(2,128)S(1)} copy(f32[1,128,2,2560]{3,1,2,0:T(8,128)S(1)} %bitcast.117) | data formatting | bytes 5242880 | tf_op jit(solution)/shard_map/all_to_all | solution.py:90
  96.9 2.0 %copy.63 = f32[16,8,2,2560]{3,1,2,0:T(8,128)} copy(f32[16,8,2,2560]{3,2,1,0:T(2,128)S(1)} %bitcast.118) | data formatting | bytes 5242880
  98.9 0.0 copy-start.5
  98.9 0.0 copy-start.6
  98.9 0.0 copy-start.7
  98.9 0.0 copy-start.2
  98.9 0.0 reduce-scatter.2.cloned.1.call-update
  98.9 0.7 copy-done.5
  99.6 0.0 copy-done.6
  99.7 0.0 copy-done.7
  99.7 36.1 %reduce-scatter.2.cloned.1.call-done = f32[128,2560]{1,0:T(8,128)} async-done(((f32[128,5120]{1,0:T(8,128)}), f32[128,2560]{1,0:T(8,128)}) %reduce-scatter.2.cloned.1.call-update) | async-done | bytes 1310736 | tf_op jit(solution)/shard_map/reduce_scatter | solution.py:98
  135.9 0.0 copy-done.2
  135.9 0.0 copy-start.1
  135.9 1.8 %fusion.29 = (f32[128]{0:T(128)S(1)}, f32[128]{0:T(128)S(1)}) fusion(f32[128,2560]{1,0:T(8,128)} %reduce-scatter.2.cloned.1.call-done, f32[2560]{0:T(1024)S(1)} %reduce.6, bf16[1,1,128,2560]{3,2,1,0:T(8,128)(2,1)S(1)} %copy-done.2), kind=kLoop, calls=%fused_computation.25 | loop fusion | flops 1965824 | bytes 1977344 | tf_op jit(solution)/shard_map/reduce_sum | solution.py:103
  137.6 4.9 %all-reduce = (f32[1,128]{1,0:T(1,128)S(1)}, f32[1,128]{1,0:T(1,128)S(1)}) all-reduce(f32[1,128]{1,0:T(1,128)S(1)} %bitcast.130, f32[1,128]{1,0:T(1,128)S(1)} %bitcast.129), channel_id=1, replica_groups=mesh['group'=2,'seq'=4,'shard'=2,'guide'=2] {'shard'}, use_global_device_ids=true, to_apply=%region_6.0 | all-reduce | flops 256 | bytes 2048 | tf_op jit(solution)/shard_map/psum | solution.py:105
  142.6 0.0 copy-done
  142.6 0.0 copy-done.1
  142.6 0.0 copy-start.8
  142.6 0.0 copy-start.4
  142.6 1.0 fusion.6
  143.7 7.8 %psum.23 = f32[4,32,64]{2,0,1:T(4,128)S(1)} all-reduce(f32[4,32,64]{2,0,1:T(4,128)S(1)} %copy.52), channel_id=1, replica_groups=mesh['group'=2,'seq'=4,'shard'=2,'guide'=2] {'shard'}, use_global_device_ids=true, to_apply=%region_7.0 | all-reduce | flops 8192 | bytes 65536 | tf_op jit(solution)/shard_map/psum | solution.py:114
  151.5 0.0 copy-done.8
  151.5 0.3 convolution_bitcast_fusion
  151.8 0.7 reshape.232
  152.5 5.0 %all-to-all-start.1 = ((f32[4,1,2048]{2,1,0:T(1,128)}), f32[4,1,2048]{2,1,0:T(1,128)S(1)}, u32[]{:S(2)}, u32[]{:S(2)}) async-start(f32[4,1,2048]{2,1,0:T(1,128)} %reshape.232), calls=%async_computation.2 | async-start | bytes 65536 | tf_op jit(solution)/shard_map/all_to_all | solution.py:127
  158.2 5.0 %all-to-all-done.1 = f32[4,1,2048]{2,1,0:T(1,128)S(1)} async-done(((f32[4,1,2048]{2,1,0:T(1,128)}), f32[4,1,2048]{2,1,0:T(1,128)S(1)}, u32[]{:S(2)}, u32[]{:S(2)}) %all-to-all-start.1) | async-done | bytes 32800 | tf_op jit(solution)/shard_map/all_to_all | solution.py:127
  163.2 0.5 broadcast.99
  163.7 0.7 reduce.10
  164.4 0.1 reshape.233
  164.5 0.1 copy.55
  164.6 3.8 %all_to_all.43 = f32[1,1,1,128,64]{3,2,1,0,4:T(1,128)S(1)} all-to-all(f32[1,1,1,128,64]{3,2,1,0,4:T(1,128)S(1)} %copy.55), channel_id=1, replica_groups=mesh['group'=2,'seq'=4,'shard'=2,'guide'=2] {'guide'}, dimensions={4} | all-to-all | bytes 65536 | tf_op jit(solution)/shard_map/all_to_all | solution.py:126
  168.4 0.0 copy-done.4
  168.4 0.6 fusion.34
  (7 shorter events, 0.2 us)
Async XLA Ops:
  6.5 136.0 %copy-start = (bf16[2560,64]{0,1:T(8,128)(2,1)S(1)}, bf16[2560,64]{0,1:T(8,128)(2,1)}, u32[]{:S(2)}) copy-start(bf16[2560,64]{0,1:T(8,128)(2,1)} %param.20) | copy-start | bytes 983044
  6.5 2.8 %copy-start.3 = (bf16[1,1,128,1280]{3,2,1,0:T(8,128)(2,1)S(1)}, bf16[1,1,128,1280]{3,2,1,0:T(8,128)(2,1)}, u32[]{:S(2)}) copy-start(bf16[1,1,128,1280]{3,2,1,0:T(8,128)(2,1)} %param.12) | copy-start | bytes 983044
  6.5 38.6 %all-gather.5.cloned.1.call-start = ((), (), s32[]{:S(2)}) async-start(), calls=%async_computation.5 | async-start | bytes 1638400 | tf_op jit(solution)/shard_map/all_gather | solution.py:76
  8.5 69.0 %all-gather.7.cloned.1.call-start = ((), (), s32[]{:S(2)}) async-start(), calls=%async_computation.6 | async-start | bytes 1638400 | tf_op jit(solution)/shard_map/all_gather | solution.py:77
  9.2 126.6 %reduce-scatter.2.cloned.1.call-start = ((), (), s32[]{:S(2)}) async-start(), calls=%async_computation.4 | async-start | bytes 3932160 | tf_op jit(solution)/shard_map/reduce_scatter | solution.py:98
  98.9 0.7 copy-start.5
  98.9 0.7 copy-start.6
  98.9 0.8 copy-start.7
  98.9 37.0 %copy-start.2 = (bf16[1,1,128,2560]{3,2,1,0:T(8,128)(2,1)S(1)}, bf16[1,1,128,2560]{3,2,1,0:T(8,128)(2,1)}, u32[]{:S(2)}) copy-start(bf16[1,1,128,2560]{3,2,1,0:T(8,128)(2,1)} %param.15) | copy-start | bytes 1966084
  135.9 6.7 %copy-start.1 = (f32[128,2560]{1,0:T(8,128)S(1)}, f32[128,2560]{1,0:T(8,128)}, u32[]{:S(2)}) copy-start(f32[128,2560]{1,0:T(8,128)} %reduce-scatter.2.cloned.1.call-done) | copy-start | bytes 3932164
  142.6 8.9 %copy-start.8 = (s32[1,4]{1,0:T(1,128)S(1)}, s32[1,4]{1,0:T(1,128)}, u32[]{:S(2)}) copy-start(s32[1,4]{1,0:T(1,128)} %param.23) | copy-start | bytes 52
  142.6 25.8 %copy-start.4 = (f32[1,1,128,32]{2,3,1,0:T(8,128)S(1)}, f32[1,1,128,32]{2,3,1,0:T(8,128)}, u32[]{:S(2)}) copy-start(f32[1,1,128,32]{2,3,1,0:T(8,128)} %param.21) | copy-start | bytes 49156
  152.5 10.7 %all-to-all-start.1 = ((f32[4,1,2048]{2,1,0:T(1,128)}), f32[4,1,2048]{2,1,0:T(1,128)S(1)}, u32[]{:S(2)}, u32[]{:S(2)}) async-start(f32[4,1,2048]{2,1,0:T(1,128)} %reshape.232), calls=%async_computation.2 | async-start | bytes 65536 | tf_op jit(solution)/shard_map/all_to_all | solution.py:127
Sparse Core Ops, SparseCore 0:
  8.9 36.1 all-gather.4
  46.7 30.7 all-gather.6
  99.0 36.7 reduce-scatter.1
where the time goes:
time: 176 us
  waiting for transfers between devices  107 us (61%)
  blocking collectives  24.6 us (14%)
  between operations  14 us (8%)
  local copies, waits for them, and re-layouts  10.7 us (6%)
  matrix products  10.1 us (6%)
  starting transfers between devices  5.09 us (3%)
  other arithmetic  3.65 us (2%)
    reduce_scatter x1, waiting for transfers between devices, on_device(): lax.psum_scatter(projected, 'shard', scatter_dimension=1, tiled=True)  36.1 us
    all_gather x1, waiting for transfers between devices, on_device(): lax.all_gather(key_vecs[0], 'seq', axis=1, tiled=True)  35.6 us
    all_gather x1, waiting for transfers between devices, on_device(): lax.all_gather(value_vecs[0], 'seq', axis=1, tiled=True)  30 us
    psum x1, blocking collectives, on_device(): predicted = lax.psum(partial_head, 'shard')  7.79 us
    all_to_all x1, blocking collectives, on_device(): lax.all_to_all(both_rows.reshape(2, row_count, half_width), 'guide', spli...  5.84 us
    unnamed x23, local copies, waits for them, and re-layouts  5.6 us
    all_to_all x1, starting transfers between devices, on_device(): lax.all_to_all(by_owner[None], 'seq', split_axis=2, concat_axis=3, tiled=...  5.01 us
    all_to_all x1, waiting for transfers between devices, on_device(): lax.all_to_all(by_owner[None], 'seq', split_axis=2, concat_axis=3, tiled=...  4.96 us
  transfers between devices with their start and end apart: 4, of which 4 were waited for; matrix products, arithmetic and copies ran while one was open for 2% of the time, Pallas kernels for 0%

commit v1 on v0

--- a/solution.py
+++ b/solution.py
@@ -124,7 +124,12 @@
     )
     weight = plan_weight(timesteps)
     arrived = lax.all_to_all(
-        lax.all_to_all(by_owner[None], "seq", split_axis=2, concat_axis=3, tiled=True),
+        jnp.concatenate(
+            lax.all_to_all(
+                jnp.stack(jnp.split(by_owner[None], lax.axis_size("seq"), 2)), "seq", 0, 0
+            ),
+            3,
+        ),
         "guide",
         split_axis=4,
         concat_axis=0,

time: 176 us -> 176 us (level)
  no operation moved by 1% of the time
where the time goes in v1:
time: 176 us
  waiting for transfers between devices  107 us (61%)
  blocking collectives  24.6 us (14%)
  between operations  14 us (8%)
  local copies, waits for them, and re-layouts  10.7 us (6%)
  matrix products  10.1 us (6%)
  starting transfers between devices  5.09 us (3%)
  other arithmetic  3.66 us (2%)
    reduce_scatter x1, waiting for transfers between devices, on_device(): lax.psum_scatter(projected, 'shard', scatter_dimension=1, tiled=True)  36.1 us
    all_gather x1, waiting for transfers between devices, on_device(): lax.all_gather(key_vecs[0], 'seq', axis=1, tiled=True)  35.6 us
    all_gather x1, waiting for transfers between devices, on_device(): lax.all_gather(value_vecs[0], 'seq', axis=1, tiled=True)  30 us
    psum x1, blocking collectives, on_device(): predicted = lax.psum(partial_head, 'shard')  7.79 us
    all_to_all x1, blocking collectives, on_device(): lax.all_to_all(both_rows.reshape(2, row_count, half_width), 'guide', spli...  5.84 us
    unnamed x23, local copies, waits for them, and re-layouts  5.6 us
    all_to_all x1, starting transfers between devices, on_device(): lax.all_to_all(jnp.stack(jnp.split(by_owner[None], lax.axis_size('seq'),...  5.01 us
    all_to_all x1, waiting for transfers between devices, on_device(): lax.all_to_all(jnp.stack(jnp.split(by_owner[None], lax.axis_size('seq'),...  4.96 us
  transfers between devices with their start and end apart: 4, of which 4 were waited for; matrix products, arithmetic and copies ran while one was open for 2% of the time, Pallas kernels for 0%

profile of v1, /device:TPU:0, one launch (start us, length us, event | category | flops | bytes accessed | tf_op | source)
XLA Modules:
  0.0 175.6 jit_solution(10513460272092350145)
XLA Ops:
  6.5 0.0 copy-start
  6.5 0.0 copy-start.3
  6.5 0.0 all-gather.5.cloned.1.call-start
  6.5 1.9 %copy.37 = bf16[1,1,128,1280]{2,3,1,0:T(8,128)(2,1)} copy(bf16[1,1,128,1280]{3,2,1,0:T(8,128)(2,1)} %param.13) | data formatting | bytes 655360 | tf_op args[1]
  8.5 0.0 all-gather.5.cloned.1.call-update
  8.5 0.0 all-gather.7.cloned.1.call-start
  8.5 0.7 all-gather.7.cloned.1.call-update
  9.2 0.0 reduce-scatter.2.cloned.1.call-start
  9.3 0.0 copy-done.3
  9.3 0.2 copy.38
  9.5 35.6 %all-gather.5.cloned.1.call-done = bf16[1,1,512,1280]{2,3,1,0:T(8,128)(2,1)} async-done(((bf16[1,1,128,1280]{2,3,1,0:T(8,128)(2,1)}), bf16[1,1,512,1280]{2,3,1,0:T(8,128)(2,1)}) %all-gather.5.cloned.1.call-update) | async-done | bytes 1310736 | tf_op jit(solution)/shard_map/all_gather | solution.py:76
  45.1 1.9 %bitcast_reduce_fusion = (f32[128,10]{0,1:T(8,128)S(1)}, f32[10,512,128]{2,1,0:T(8,128)S(1)}) fusion(bf16[512,10,128]{0,2,1:T(8,128)(2,1)} %bitcast.126, bf16[128,10,128]{0,2,1:T(8,128)(2,1)S(1)} %bitcast.125), kind=kOutput, calls=%fused_computation.1 | convolution fusion | flops 169081600 | bytes 4264960 | tf_op jit(solution)/shard_map/tqhd,tkhd->tqhk/dot_general | solution.py:30
  47.0 0.4 fusion.1
  47.5 30.0 %all-gather.7.cloned.1.call-done = bf16[1,1,512,1280]{3,2,1,0:T(8,128)(2,1)} async-done(((bf16[1,1,128,1280]{3,2,1,0:T(8,128)(2,1)}), bf16[1,1,512,1280]{3,2,1,0:T(8,128)(2,1)}) %all-gather.7.cloned.1.call-update) | async-done | bytes 1310736 | tf_op jit(solution)/shard_map/all_gather | solution.py:77
  77.5 2.4 %copy.41 = bf16[1,1,512,1280]{2,3,1,0:T(8,128)(2,1)} copy(bf16[1,1,512,1280]{3,2,1,0:T(8,128)(2,1)} %all-gather.7.cloned.1.call-done) | data formatting | bytes 2621440 | tf_op jit(solution)/shard_map/all_gather | solution.py:77
  79.9 2.1 %fusion.22 = bf16[1,128,10,128]{1,3,2,0:T(8,128)(2,1)S(1)} fusion(bf16[512,10,128]{0,2,1:T(8,128)(2,1)} %bitcast.127, f32[10,512,128]{2,1,0:T(8,128)S(1)} %get-tuple-element.18, f32[128,10]{0,1:T(8,128)S(1)} %get-tuple-element.17, f32[128,10]{0,1:T(8,128)S(1)} %get-tuple-element.14, f32[128,10]{0,1:T(8,128)S(1)} %get-tuple-element.13), kind=kOutput, calls=%fused_computation.19 | convolution fusion | flops 170229760 | bytes 4275200 | tf_op jit(solution)/shard_map/tqhk,tkhd->tqhd/dot_general | solution.py:37
  82.0 2.3 %all_gather.11 = bf16[256,1280]{0,1:T(8,128)(2,1)S(1)} all-gather(bf16[128,1280]{0,1:T(8,128)(2,1)S(1)} %bitcast.128), channel_id=1, replica_groups=mesh['group'=2,'seq'=4,'shard'=2,'guide'=2] {'guide'}, dimensions={0}, use_global_device_ids=true | all-gather | bytes 983040 | tf_op jit(solution)/shard_map/all_gather | solution.py:85
  84.3 4.7 %fusion.41 = f32[256,2560]{1,0:T(8,128)S(1)} fusion(bf16[256,1280]{0,1:T(8,128)(2,1)S(1)} %all_gather.11, bf16[1280,2560]{1,0:T(8,128)(2,1)} %param.16), kind=kOutput, calls=%fused_computation.44 | convolution fusion | flops 1677721600 | bytes 9830400 | tf_op jit(solution)/shard_map/dot_general | solution.py:84
  89.1 5.8 %all_to_all.35 = f32[2,128,2560]{2,1,0:T(8,128)S(1)} all-to-all(f32[2,128,2560]{2,1,0:T(8,128)S(1)} %bitcast.121), channel_id=1, replica_groups=mesh['group'=2,'seq'=4,'shard'=2,'guide'=2] {'guide'}, dimensions={0} | all-to-all | bytes 5242880 | tf_op jit(solution)/shard_map/all_to_all | solution.py:90
  94.9 2.0 %copy.43 = f32[1,128,2,2560]{3,2,1,0:T(2,128)S(1)} copy(f32[1,128,2,2560]{3,1,2,0:T(8,128)S(1)} %bitcast.123) | data formatting | bytes 5242880 | tf_op jit(solution)/shard_map/all_to_all | solution.py:90
  96.9 2.0 %copy.61 = f32[16,8,2,2560]{3,1,2,0:T(8,128)} copy(f32[16,8,2,2560]{3,2,1,0:T(2,128)S(1)} %bitcast.124) | data formatting | bytes 5242880
  98.9 0.0 copy-start.5
  98.9 0.0 copy-start.6
  98.9 0.0 copy-start.7
  98.9 0.0 copy-start.2
  98.9 0.0 reduce-scatter.2.cloned.1.call-update
  98.9 0.7 copy-done.5
  99.6 0.0 copy-done.6
  99.7 0.0 copy-done.7
  99.7 36.1 %reduce-scatter.2.cloned.1.call-done = f32[128,2560]{1,0:T(8,128)} async-done(((f32[128,5120]{1,0:T(8,128)}), f32[128,2560]{1,0:T(8,128)}) %reduce-scatter.2.cloned.1.call-update) | async-done | bytes 1310736 | tf_op jit(solution)/shard_map/reduce_scatter | solution.py:98
  135.9 0.0 copy-done.2
  135.9 0.0 copy-start.1
  135.9 1.8 %fusion.29 = (f32[128]{0:T(128)S(1)}, f32[128]{0:T(128)S(1)}) fusion(f32[128,2560]{1,0:T(8,128)} %reduce-scatter.2.cloned.1.call-done, f32[2560]{0:T(1024)S(1)} %reduce.6, bf16[1,1,128,2560]{3,2,1,0:T(8,128)(2,1)S(1)} %copy-done.2), kind=kLoop, calls=%fused_computation.25 | loop fusion | flops 1965824 | bytes 1977344 | tf_op jit(solution)/shard_map/reduce_sum | solution.py:103
  137.6 4.9 %all-reduce = (f32[1,128]{1,0:T(1,128)S(1)}, f32[1,128]{1,0:T(1,128)S(1)}) all-reduce(f32[1,128]{1,0:T(1,128)S(1)} %bitcast.138, f32[1,128]{1,0:T(1,128)S(1)} %bitcast.137), channel_id=1, replica_groups=mesh['group'=2,'seq'=4,'shard'=2,'guide'=2] {'shard'}, use_global_device_ids=true, to_apply=%region_6.0 | all-reduce | flops 256 | bytes 2048 | tf_op jit(solution)/shard_map/psum | solution.py:105
  142.6 0.0 copy-done
  142.6 0.0 copy-done.1
  142.6 0.0 copy-start.8
  142.6 0.0 copy-start.4
  142.6 1.0 fusion.6
  143.7 7.8 %psum.23 = f32[4,32,64]{2,0,1:T(4,128)S(1)} all-reduce(f32[4,32,64]{2,0,1:T(4,128)S(1)} %copy.45), channel_id=1, replica_groups=mesh['group'=2,'seq'=4,'shard'=2,'guide'=2] {'shard'}, use_global_device_ids=true, to_apply=%region_7.0 | all-reduce | flops 8192 | bytes 65536 | tf_op jit(solution)/shard_map/psum | solution.py:114
  151.5 0.0 copy-done.8
  151.5 0.3 convolution_bitcast_fusion
  151.9 0.7 reshape.233
  152.6 5.0 %all-to-all-start.1 = ((f32[4,1,2048]{2,1,0:T(1,128)}), f32[4,1,2048]{2,1,0:T(1,128)S(1)}, u32[]{:S(2)}, u32[]{:S(2)}) async-start(f32[4,1,2048]{2,1,0:T(1,128)} %reshape.233), calls=%async_computation.2 | async-start | bytes 65536 | tf_op jit(solution)/shard_map/all_to_all | solution.py:128
  158.3 5.0 %all-to-all-done.1 = f32[4,1,2048]{2,1,0:T(1,128)S(1)} async-done(((f32[4,1,2048]{2,1,0:T(1,128)}), f32[4,1,2048]{2,1,0:T(1,128)S(1)}, u32[]{:S(2)}, u32[]{:S(2)}) %all-to-all-start.1) | async-done | bytes 32800 | tf_op jit(solution)/shard_map/all_to_all | solution.py:128
  163.3 0.5 broadcast.99
  163.8 0.7 reduce.10
  164.5 0.1 reshape.234
  164.6 0.1 copy.50
  164.7 3.8 %all_to_all.36 = f32[1,1,1,128,64]{3,2,1,0,4:T(1,128)S(1)} all-to-all(f32[1,1,1,128,64]{3,2,1,0,4:T(1,128)S(1)} %copy.50), channel_id=1, replica_groups=mesh['group'=2,'seq'=4,'shard'=2,'guide'=2] {'guide'}, dimensions={4} | all-to-all | bytes 65536 | tf_op jit(solution)/shard_map/all_to_all | solution.py:126
  168.4 0.0 copy-done.4
  168.4 0.6 fusion.34
  (8 shorter events, 0.2 us)
Async XLA Ops:
  6.5 136.0 %copy-start = (bf16[2560,64]{0,1:T(8,128)(2,1)S(1)}, bf16[2560,64]{0,1:T(8,128)(2,1)}, u32[]{:S(2)}) copy-start(bf16[2560,64]{0,1:T(8,128)(2,1)} %param.20) | copy-start | bytes 983044
  6.5 2.8 %copy-start.3 = (bf16[1,1,128,1280]{3,2,1,0:T(8,128)(2,1)S(1)}, bf16[1,1,128,1280]{3,2,1,0:T(8,128)(2,1)}, u32[]{:S(2)}) copy-start(bf16[1,1,128,1280]{3,2,1,0:T(8,128)(2,1)} %param.12) | copy-start | bytes 983044
  6.5 38.6 %all-gather.5.cloned.1.call-start = ((), (), s32[]{:S(2)}) async-start(), calls=%async_computation.5 | async-start | bytes 1638400 | tf_op jit(solution)/shard_map/all_gather | solution.py:76
  8.5 69.0 %all-gather.7.cloned.1.call-start = ((), (), s32[]{:S(2)}) async-start(), calls=%async_computation.6 | async-start | bytes 1638400 | tf_op jit(solution)/shard_map/all_gather | solution.py:77
  9.2 126.6 %reduce-scatter.2.cloned.1.call-start = ((), (), s32[]{:S(2)}) async-start(), calls=%async_computation.4 | async-start | bytes 3932160 | tf_op jit(solution)/shard_map/reduce_scatter | solution.py:98
  98.9 0.7 copy-start.5
  98.9 0.7 copy-start.6
  98.9 0.8 copy-start.7
  98.9 37.0 %copy-start.2 = (bf16[1,1,128,2560]{3,2,1,0:T(8,128)(2,1)S(1)}, bf16[1,1,128,2560]{3,2,1,0:T(8,128)(2,1)}, u32[]{:S(2)}) copy-start(bf16[1,1,128,2560]{3,2,1,0:T(8,128)(2,1)} %param.15) | copy-start | bytes 1966084
  135.9 6.7 %copy-start.1 = (f32[128,2560]{1,0:T(8,128)S(1)}, f32[128,2560]{1,0:T(8,128)}, u32[]{:S(2)}) copy-start(f32[128,2560]{1,0:T(8,128)} %reduce-scatter.2.cloned.1.call-done) | copy-start | bytes 3932164
  142.6 8.9 %copy-start.8 = (s32[1,4]{1,0:T(1,128)S(1)}, s32[1,4]{1,0:T(1,128)}, u32[]{:S(2)}) copy-start(s32[1,4]{1,0:T(1,128)} %param.23) | copy-start | bytes 52
  142.6 25.8 %copy-start.4 = (f32[1,1,128,32]{2,3,1,0:T(8,128)S(1)}, f32[1,1,128,32]{2,3,1,0:T(8,128)}, u32[]{:S(2)}) copy-start(f32[1,1,128,32]{2,3,1,0:T(8,128)} %param.21) | copy-start | bytes 49156
  152.6 10.7 %all-to-all-start.1 = ((f32[4,1,2048]{2,1,0:T(1,128)}), f32[4,1,2048]{2,1,0:T(1,128)S(1)}, u32[]{:S(2)}, u32[]{:S(2)}) async-start(f32[4,1,2048]{2,1,0:T(1,128)} %reshape.233), calls=%async_computation.2 | async-start | bytes 65536 | tf_op jit(solution)/shard_map/all_to_all | solution.py:128
Sparse Core Ops, SparseCore 0:
  8.9 36.1 all-gather.4
  46.7 30.7 all-gather.6
  99.0 36.7 reduce-scatter.1
